TPU v7x, 32 devices: a whole 2x2x4 slice. The times are simulated.
32 devices in a mesh: row: 4 (over x, core), col: 8 (over z, y).
Axes of the slice: x: 2, y: 2, z: 4, core: 2. Of those that a mesh axis runs over, the one named last changes fastest.
Arguments:
- residual: bfloat16 [30720, 512], P('row', 'col'), may hold values from -4 to 4
- interaction: bfloat16 [30720, 5120], P('row', 'col'), may hold values from -0.078125 to 0.078125
- commands: bfloat16 [5120, 512], P('col'), may hold values from -6 to 6
- slope_valid: int32 [240], P('row'), may hold values 0 or 1
- frame_valid: int32 [512], P('col'), may hold values 0 or 1
Outputs:
- covariance: bfloat16 [30720, 30720], P('row', 'col')
All inputs are finite; a program needn't handle non-finite values. No bound on the sum of `slope_valid` or of `frame_valid` on one device may be relied on, other than what follows from the above.
Results may differ from a plain program's by a relative error of at most 0.02.
Values may be sent and summed in bfloat16 or wider, within the bound.
A program may use at most 128 MiB of HBM per device.

v0:
```python
import jax
import jax.numpy as jnp
from jax import lax
from jax.sharding import PartitionSpec as P

SBLK = 128
FRAMES = 512


def per_device(residual, interaction, commands, slope_valid, frame_valid):
    block_rows = interaction.shape[0]
    product = jnp.dot(interaction, commands, preferred_element_type=jnp.float32)
    summed = lax.psum_scatter(
        product.astype(jnp.bfloat16), "col", scatter_dimension=1, tiled=True
    ).astype(jnp.float32)
    row_mask = (
        (slope_valid[:, None] * jnp.ones((1, SBLK), jnp.int32)).reshape(-1).astype(jnp.float32)
    )
    local_slopes = (
        (residual.astype(jnp.float32) + summed)
        * row_mask[:, None]
        * frame_valid[None, :].astype(jnp.float32)
    ).astype(jnp.bfloat16)
    row_copy = lax.all_gather(local_slopes, "col", axis=1, tiled=True)
    total_slopes = block_rows * lax.axis_size("row")
    block_cols = total_slopes // lax.axis_size("col")
    col_index = lax.axis_index("col")
    gathered = lax.all_gather(local_slopes, "row", axis=0, tiled=True)
    columns = lax.all_to_all(gathered, "col", split_axis=0, concat_axis=1, tiled=True)
    row_start = lax.axis_index("row") * block_rows
    col_start = col_index * block_cols
    row_ids = row_start + jnp.arange(block_rows, dtype=jnp.int32)[:, None]
    col_ids = col_start + jnp.arange(block_cols, dtype=jnp.int32)[None, :]
    tile = (
        lax.dot_general(
            row_copy, columns, (((1,), (1,)), ((), ())), preferred_element_type=jnp.float32
        )
        / FRAMES
    )
    return jnp.where(row_ids <= col_ids, tile, jnp.float32(0.0)).astype(jnp.bfloat16)


def solution(mesh):
    placed = (P("row", "col"), P("row", "col"), P("col", None), P("row"), P("col"))
    return jax.shard_map(
        per_device, mesh=mesh, in_specs=placed, out_specs=P("row", "col"), check_vma=False
    )
```

profile of v0, /device:TPU:17, one launch (start us, length us, event | category | flops | bytes accessed | tf_op | source)
XLA Modules:
  0.0 434.8 jit_solution(12325479524292359693)
XLA Ops:
  6.5 0.0 copy-start
  6.5 0.0 reduce-scatter.2.cloned.1.call-start
  6.5 1.1 copy-done
  7.6 10.9 %convolution_convert_fusion = bf16[7680,512]{0,1:T(8,128)(2,1)} fusion(bf16[7680,640]{1,0:T(8,128)(2,1)} %param.6, bf16[640,512]{1,0:T(8,128)(2,1)S(1)} %copy-done), kind=kOutput, calls=%fused_computation.1 | convolution fusion | flops 5037096960 | bytes 18350080 | tf_op jit(solution)/shard_map/dot_general | solution.py:12
  18.5 0.0 copy-start.3
  18.5 0.0 copy-start.4
  18.5 0.0 copy-start.2
  18.5 0.0 reduce-scatter.2.cloned.1.call-update
  18.5 0.0 all-gather.5.cloned.1.call-start
  18.6 0.6 copy-done.3
  19.1 0.0 copy-done.4
  19.2 0.1 broadcast_bitcast_fusion
  19.2 140.1 %reduce-scatter.2.cloned.1.call-done = bf16[7680,64]{0,1:T(8,128)(2,1)} async-done(((bf16[7680,512]{0,1:T(8,128)(2,1)}), bf16[7680,64]{0,1:T(8,128)(2,1)}) %reduce-scatter.2.cloned.1.call-update) | async-done | bytes 983056 | tf_op jit(solution)/shard_map/reduce_scatter | solution.py:13
  159.3 0.0 copy-done.2
  159.3 2.5 multiply_convert_fusion
  161.9 0.0 all-gather.5.cloned.1.call-update
  161.9 0.0 all-gather.3.cloned.1.call-start
  161.9 0.7 all-gather.3.cloned.1.call-update
  162.6 32.8 %all-gather.5.cloned.1.call-done = bf16[30720,64]{0,1:T(8,128)(2,1)} async-done(((bf16[7680,64]{0,1:T(8,128)(2,1)}), bf16[30720,64]{0,1:T(8,128)(2,1)}) %all-gather.5.cloned.1.call-update) | async-done | bytes 3932176 | tf_op jit(solution)/shard_map/all_gather | solution.py:28
  195.5 4.3 copy.9
  199.8 5.5 %all-to-all-start = ((bf16[8,3840,64]{1,2,0:T(8,128)(2,1)}), bf16[8,3840,64]{1,2,0:T(8,128)(2,1)}, u32[]{:S(2)}, u32[]{:S(2)}) async-start(bf16[8,3840,64]{1,2,0:T(8,128)(2,1)} %bitcast.13), calls=%async_computation.1 | async-start | bytes 7864320 | tf_op jit(solution)/shard_map/all_to_all | solution.py:29
  205.3 163.9 %all-to-all-done = bf16[8,3840,64]{1,2,0:T(8,128)(2,1)} async-done(((bf16[8,3840,64]{1,2,0:T(8,128)(2,1)}), bf16[8,3840,64]{1,2,0:T(8,128)(2,1)}, u32[]{:S(2)}, u32[]{:S(2)}) %all-to-all-start) | async-done | bytes 3932192 | tf_op jit(solution)/shard_map/all_to_all | solution.py:29
  369.2 16.3 %all-gather.3.cloned.1.call-done = bf16[7680,512]{0,1:T(8,128)(2,1)} async-done(((bf16[7680,64]{0,1:T(8,128)(2,1)}), bf16[7680,512]{0,1:T(8,128)(2,1)}) %all-gather.3.cloned.1.call-update) | async-done | bytes 7864336 | tf_op jit(solution)/shard_map/all_gather | solution.py:24
  385.5 0.0 copy-start.1
  385.5 42.8 %select_convert_fusion = bf16[7680,3840]{1,0:T(8,128)(2,1)} fusion(bf16[7680,512]{0,1:T(8,128)(2,1)} %all-gather.3.cloned.1.call-done, bf16[3840,512]{0,1:T(8,128)(2,1)} %bitcast.2, s32[3840]{0:T(1024)S(1)} %iota_add_fusion.1, s32[7680]{0:T(1024)S(1)} %iota_add_fusion), kind=kOutput, calls=%fused_computation | convolution fusion | flops 30316953600 | bytes 70824960 | tf_op jit(solution)/shard_map/dot_general | solution.py:35
  428.3 0.0 copy-done.1
  (4 shorter events, 0.0 us)
Async XLA Ops:
  6.5 1.1 copy-start
  6.5 152.8 %reduce-scatter.2.cloned.1.call-start = ((), (), s32[]{:S(2)}) async-start(), calls=%async_computation.2 | async-start | bytes 8847360 | tf_op jit(solution)/shard_map/reduce_scatter | solution.py:13
  18.5 0.7 copy-start.3
  18.5 0.7 copy-start.4
  18.5 140.8 %copy-start.2 = (bf16[7680,64]{0,1:T(8,128)(2,1)S(1)}, bf16[7680,64]{0,1:T(8,128)(2,1)}, u32[]{:S(2)}) copy-start(bf16[7680,64]{0,1:T(8,128)(2,1)} %param.5) | copy-start | bytes 2949124
  18.5 177.0 %all-gather.5.cloned.1.call-start = ((), (), s32[]{:S(2)}) async-start(), calls=%async_computation.4 | async-start | bytes 4915200 | tf_op jit(solution)/shard_map/all_gather | solution.py:28
  161.9 223.6 %all-gather.3.cloned.1.call-start = ((), (), s32[]{:S(2)}) async-start(), calls=%async_computation.3 | async-start | bytes 8847360 | tf_op jit(solution)/shard_map/all_gather | solution.py:24
  199.8 169.4 %all-to-all-start = ((bf16[8,3840,64]{1,2,0:T(8,128)(2,1)}), bf16[8,3840,64]{1,2,0:T(8,128)(2,1)}, u32[]{:S(2)}, u32[]{:S(2)}) async-start(bf16[8,3840,64]{1,2,0:T(8,128)(2,1)} %bitcast.13), calls=%async_computation.1 | async-start | bytes 7864320 | tf_op jit(solution)/shard_map/all_to_all | solution.py:29
  385.5 42.8 %copy-start.1 = (bf16[640,512]{1,0:T(8,128)(2,1)S(1)}, bf16[640,512]{1,0:T(8,128)(2,1)}, u32[]{:S(2)}) copy-start(bf16[640,512]{1,0:T(8,128)(2,1)} %param.7) | copy-start | bytes 1966084
Sparse Core Ops, SparseCore 0:
  18.6 140.6 reduce-scatter.1
  162.0 33.4 all-gather.4
  197.7 187.7 all-gather.2
where the time goes:
time: 441 us; the launch traced here: 435 us
  waiting for transfers between devices  354 us (80%)
  matrix products  53.6 us (12%)
  between operations  13.1 us (3%)
  local copies, waits for them, and re-layouts  6.07 us (1%)
  starting transfers between devices  5.56 us (1%)
    all_to_all x1, waiting for transfers between devices, per_device(): lax.all_to_all(gathered, 'col', split_axis=0, concat_axis=1, tiled=True)  164 us
    reduce_scatter x1, waiting for transfers between devices, per_device(): lax.psum_scatter(product.astype(jnp.bfloat16), 'col', scatter_dimension=1...  140 us
    dot_general x1, matrix products, per_device(): lax.dot_general(row_copy, columns, (((1,), (1,)), ((), ())), preferred_el...  42.8 us
    all_gather x1, waiting for transfers between devices, per_device(): gathered = lax.all_gather(local_slopes, 'row', axis=0, tiled=True)  32.8 us
    all_gather x1, waiting for transfers between devices, per_device(): row_copy = lax.all_gather(local_slopes, 'col', axis=1, tiled=True)  16.3 us
    dot_general x1, matrix products, per_device(): product = jnp.dot(interaction, commands, preferred_element_type=jnp.float32)  10.9 us
  transfers between devices with their start and end apart: 4, of which 4 were waited for; matrix products, arithmetic and copies ran while one was open for 1% of the time, Pallas kernels for 0%

commit v1 on v0

v1 whole, which is shorter than its diff:
```python
import functools

import jax
import jax.numpy as jnp
from jax import lax
from jax.experimental import pallas as pl
from jax.experimental.pallas import tpu as pltpu
from jax.sharding import PartitionSpec as P

SBLK = 128
MESH = pl.DeviceIdType.MESH
LANES = 4


def divisor(n, limit, unit):
    best = n
    for d in range(unit, min(n, limit) + 1, unit):
        if n % d == 0:
            best = d
    return best


def ring_position(c, n):
    return lax.rem(c + 1, 2) * (c // 2) + lax.rem(c, 2) * (n - 1 - c // 2)


def ring_column(p, n):
    up = 2 * p
    down = 2 * (n - 1 - p) + 1
    return jnp.where(p < n // 2, up, down)


def comm_kernel(
    C, R, rows, fl, inter_hbm, resid_hbm, cmd_ref, sel_ref, rmask_ref, fmask_ref,
    s_hbm, col_hbm,
    inter, resid, stage, recv, own, fall,
    in_sem, rs_send, rs_recv, ag_send, ag_recv, m_send, m_recv, c_send, c_recv, own_sem,
):
    r = lax.axis_index("row")
    c = lax.axis_index("col")
    p = ring_position(c, C)
    nxt = ring_column(lax.rem(p + 1, C), C)
    prv = ring_column(lax.rem(p + C - 1, C), C)
    br = C * rows
    bc = br * R // C
    per_row = br // bc
    rc = c // per_row
    k0 = lax.rem(c, per_row) * (bc // rows)
    nk = bc // rows
    tile = divisor(rows, 256, 16)

    def load(k):
        return (
            pltpu.make_async_copy(inter_hbm.at[k], inter.at[k], in_sem.at[0, k]),
            pltpu.make_async_copy(resid_hbm.at[k], resid.at[k], in_sem.at[1, k]),
        )

    def start_load(k):
        for cp in load(k):
            cp.start()

    def wait_load(k):
        for cp in load(k):
            cp.wait()

    for i in range(1, C // 2):
        start_load(lax.rem(p + C - i, C))
        start_load(lax.rem(p + i, C))
    start_load(lax.rem(p + C // 2, C))
    start_load(p)

    barrier = pltpu.get_barrier_semaphore()
    for j in range(1, C):
        pl.semaphore_signal(
            barrier, inc=1, device_id=(r, lax.rem(c + j, C)), device_id_type=MESH
        )
    for j in range(1, R):
        pl.semaphore_signal(
            barrier, inc=1, device_id=(lax.rem(r + j, R), c), device_id_type=MESH
        )
    pl.semaphore_wait(barrier, C - 1 + R - 1)

    def mask_copy(j):
        return pltpu.make_async_remote_copy(
            src_ref=fmask_ref, dst_ref=fall.at[j - 1],
            send_sem=m_send.at[j - 1], recv_sem=m_recv.at[j - 1],
            device_id=(r, lax.rem(c + j, C)), device_id_type=MESH,
        )

    for j in range(1, C):
        mask_copy(j).start()

    def lane_is_up(l):
        return l < LANES // 2

    def rs_chunk(l, s):
        if lane_is_up(l):
            return lax.rem(p + 2 * C - 1 - s, C)
        return lax.rem(p + 1 + s, C)

    def ag_chunk(l, s):
        if lane_is_up(l):
            return lax.rem(p + 2 * C - s, C)
        return lax.rem(p + s, C)

    def rs_copy(l, s):
        return pltpu.make_async_remote_copy(
            src_ref=stage.at[l, s], dst_ref=recv.at[l, s],
            send_sem=rs_send.at[l, s], recv_sem=rs_recv.at[l, s],
            device_id=(r, nxt if lane_is_up(l) else prv), device_id_type=MESH,
        )

    def partial(l, k, t):
        at = pl.ds(pl.multiple_of(t * tile, 8), tile)
        cols = slice(l * fl, (l + 1) * fl)
        return jnp.dot(
            inter[k, at, :], cmd_ref[:, cols], preferred_element_type=jnp.float32
        ) + jnp.dot(
            resid[k, at, :], sel_ref[:, cols], preferred_element_type=jnp.float32
        )

    def rs_step(s, first):
        for l in range(LANES):
            k = rs_chunk(l, s)
            if not first:
                rs_copy(l, s - 1).wait_recv()

            def one(t, _, l=l, k=k):
                at = pl.ds(pl.multiple_of(t * tile, 8), tile)
                value = partial(l, k, t)
                if not first:
                    value = value + recv[l, s - 1, at, :].astype(jnp.float32)
                stage[l, s, at, :] = value.astype(jnp.bfloat16)
                return 0

            lax.fori_loop(0, rows // tile, one, 0)
            rs_copy(l, s).start()

    for s in range(C - 1):
        i = s + 1
        if i < C // 2:
            wait_load(lax.rem(p + C - i, C))
            wait_load(lax.rem(p + i, C))
        elif i == C // 2:
            wait_load(lax.rem(p + C // 2, C))
            wait_load(p)
        if s <= C // 2:
            rs_step(s, s == 0)
    if C - 1 > C // 2 + 1:
        lax.fori_loop(C // 2 + 1, C - 1, lambda s, _: (rs_step(s, False), 0)[1], 0)

    for j in range(1, C):
        mask_copy(j).wait_recv()
    frames = fmask_ref[...]
    for j in range(1, C):
        frames = frames + fall[j - 1]

    def ag_copy(l, s, from_own=False):
        k = ag_chunk(l, s)
        return pltpu.make_async_remote_copy(
            src_ref=own.at[l] if from_own else s_hbm.at[l, k],
            dst_ref=s_hbm.at[l, k],
            send_sem=ag_send.at[l, s], recv_sem=ag_recv.at[l, s],
            device_id=(r, nxt if lane_is_up(l) else prv), device_id_type=MESH,
        )

    def own_copy(l):
        return pltpu.make_async_copy(own.at[l], s_hbm.at[l, p], own_sem.at[l])

    for l in range(LANES):
        rs_copy(l, C - 2).wait_recv()

        def last(t, _, l=l):
            at = pl.ds(pl.multiple_of(t * tile, 8), tile)
            value = partial(l, p, t) + recv[l, C - 2, at, :].astype(jnp.float32)
            value = value * rmask_ref[p, at, :] * frames[0:1, l * fl:(l + 1) * fl]
            own[l, at, :] = value.astype(jnp.bfloat16)
            return 0

        lax.fori_loop(0, rows // tile, last, 0)
        ag_copy(l, 0, True).start()
        own_copy(l).start()

    def down(l, k):
        return pltpu.make_async_remote_copy(
            src_ref=col_hbm.at[l, k - k0], dst_ref=col_hbm.at[l, k - k0],
            send_sem=c_send.at[l, k - k0], recv_sem=c_recv.at[l, k - k0],
            device_id=(lax.rem(r + R - 1, R), c), device_id_type=MESH,
        )

    def down_first(l, k):
        return pltpu.make_async_remote_copy(
            src_ref=s_hbm.at[l, k], dst_ref=col_hbm.at[l, k - k0],
            send_sem=c_send.at[l, k - k0], recv_sem=c_recv.at[l, k - k0],
            device_id=(lax.rem(r + R - 1, R), c), device_id_type=MESH,
        )

    def chain(u):
        t = u - (rc - r)
        for l in range(LANES):
            if lane_is_up(l):
                k = lax.rem(p + 4 * C * R - t, C)
            else:
                k = lax.rem(p + 4 * C * R + t, C)
            live = (t >= 0) & (t < C) & (r <= rc) & (k >= k0) & (k < k0 + nk)

            @pl.when(live & (r < rc))
            def _(l=l, k=k):
                down(l, k).wait_recv()

            @pl.when(live & (r > 0) & (r < rc))
            def _(l=l, k=k):
                down(l, k).start()

            @pl.when(live & (r > 0) & (r == rc))
            def _(l=l, k=k):
                down_first(l, k).start()

    for l in range(LANES):
        own_copy(l).wait()
    chain(0)

    def ag_step(s, _):
        for l in range(LANES):
            ag_copy(l, s - 1).wait_recv()
            ag_copy(l, s).start()
        chain(s)
        return 0

    lax.fori_loop(1, C - 1, ag_step, 0)
    for l in range(LANES):
        ag_copy(l, C - 2).wait_recv()

    lax.fori_loop(C - 1, C + R - 1, lambda u, _: (chain(u), 0)[1], 0)

    def drain(s, _):
        for l in range(LANES):
            rs_copy(l, s).wait_send()
            ag_copy(l, s).wait_send()
        return 0

    lax.fori_loop(0, C - 1, drain, 0)
    for j in range(1, C):
        mask_copy(j).wait_send()

    def drain_down(i, _):
        for l in range(LANES):
            @pl.when((r > 0) & (r <= rc))
            def _(l=l):
                down(l, k0 + i).wait_send()
        return 0

    lax.fori_loop(0, nk, drain_down, 0)


def cov_kernel(C, R, br, bc, F, tm, tn, rows_ref, s_hbm, col_hbm, out_ref, cols, sem):
    r = lax.axis_index("row")
    c = lax.axis_index("col")
    i = pl.program_id(0)
    per_row = br // bc
    rc = c // per_row
    fl = F // LANES

    @pl.when(i == 0)
    def _():
        def copies(src):
            return [
                pltpu.make_async_copy(
                    src(l), cols.at[:, pl.ds(l * fl, fl)], sem.at[l]
                )
                for l in range(LANES)
            ]

        start = lax.rem(c, per_row) * bc

        @pl.when(r == rc)
        def _():
            cps = copies(lambda l: s_hbm.at[l, pl.ds(pl.multiple_of(start, 8), bc), :])
            for cp in cps:
                cp.start()
            for cp in cps:
                cp.wait()

        @pl.when(r < rc)
        def _():
            cps = copies(lambda l: col_hbm.at[l])
            for cp in cps:
                cp.start()
            for cp in cps:
                cp.wait()

    row0 = r * br + i * tm
    for j in range(bc // tn):
        col0 = c * bc + j * tn
        at = slice(j * tn, (j + 1) * tn)

        @pl.when(row0 >= col0 + tn)
        def _(at=at):
            out_ref[:, at] = jnp.zeros((tm, tn), jnp.bfloat16)

        def value(at=at):
            a = jnp.concatenate([rows_ref[l] for l in range(LANES)], axis=1)
            return lax.dot_general(
                a, cols[at, :], (((1,), (1,)), ((), ())),
                preferred_element_type=jnp.float32,
            ) / F

        @pl.when(row0 + tm <= col0)
        def _(at=at, value=value):
            out_ref[:, at] = value().astype(jnp.bfloat16)

        @pl.when((row0 < col0 + tn) & (row0 + tm > col0))
        def _(at=at, value=value, col0=col0):
            rid = row0 + lax.broadcasted_iota(jnp.int32, (tm, tn), 0)
            cid = col0 + lax.broadcasted_iota(jnp.int32, (tm, tn), 1)
            out_ref[:, at] = jnp.where(rid <= cid, value(), 0.0).astype(jnp.bfloat16)


def per_device(R, C, residual, interaction, commands, slope_valid, frame_valid):
    br, kd = interaction.shape
    F = commands.shape[1]
    fc = residual.shape[1]
    rows = br // C
    fl = F // LANES
    bc = br * R // C
    c = lax.axis_index("col")
    own_col = (
        c * fc + jnp.arange(fc, dtype=jnp.int32)[:, None]
        == jnp.arange(F, dtype=jnp.int32)[None, :]
    )
    sel = own_col.astype(jnp.bfloat16)
    fmask = jnp.sum(
        jnp.where(own_col, frame_valid[:, None], 0), axis=0, dtype=jnp.int32
    ).astype(jnp.float32)
    fmask = jnp.broadcast_to(fmask[None, :], (8, F))
    rmask = jnp.broadcast_to(slope_valid.astype(jnp.float32)[:, None], (br // SBLK, SBLK))
    rmask = rmask.reshape(C, rows, 1)
    any_spec = pl.BlockSpec(memory_space=pl.ANY)
    vmem = pl.BlockSpec(memory_space=pltpu.VMEM)
    nk = bc // rows
    slopes, colsl = pl.pallas_call(
        functools.partial(comm_kernel, C, R, rows, fl),
        out_shape=[
            jax.ShapeDtypeStruct((LANES, C, rows, fl), jnp.bfloat16),
            jax.ShapeDtypeStruct((LANES, nk, rows, fl), jnp.bfloat16),
        ],
        in_specs=[any_spec, any_spec, vmem, vmem, vmem, vmem],
        out_specs=[any_spec, any_spec],
        scratch_shapes=[
            pltpu.VMEM((C, rows, kd), jnp.bfloat16),
            pltpu.VMEM((C, rows, fc), jnp.bfloat16),
            pltpu.VMEM((LANES, C - 1, rows, fl), jnp.bfloat16),
            pltpu.VMEM((LANES, C - 1, rows, fl), jnp.bfloat16),
            pltpu.VMEM((LANES, rows, fl), jnp.bfloat16),
            pltpu.VMEM((C - 1, 8, F), jnp.float32),
            pltpu.SemaphoreType.DMA((2, C)),
            pltpu.SemaphoreType.DMA((LANES, C - 1)),
            pltpu.SemaphoreType.DMA((LANES, C - 1)),
            pltpu.SemaphoreType.DMA((LANES, C - 1)),
            pltpu.SemaphoreType.DMA((LANES, C - 1)),
            pltpu.SemaphoreType.DMA((C - 1,)),
            pltpu.SemaphoreType.DMA((C - 1,)),
            pltpu.SemaphoreType.DMA((LANES, nk)),
            pltpu.SemaphoreType.DMA((LANES, nk)),
            pltpu.SemaphoreType.DMA((LANES,)),
        ],
        compiler_params=pltpu.CompilerParams(
            collective_id=0, has_side_effects=True, vmem_limit_bytes=56 * 1024 * 1024
        ),
        name="slopes_ring",
    )(
        interaction.reshape(C, rows, kd), residual.reshape(C, rows, fc),
        commands, sel, rmask, fmask,
    )
    slopes = slopes.reshape(LANES, br, fl)
    colsl = colsl.reshape(LANES, bc, fl)
    tm = divisor(br, 256, 16)
    tn = divisor(bc, 768, 128)
    return pl.pallas_call(
        functools.partial(cov_kernel, C, R, br, bc, F, tm, tn),
        grid=(br // tm,),
        out_shape=jax.ShapeDtypeStruct((br, bc), jnp.bfloat16),
        in_specs=[
            pl.BlockSpec((LANES, tm, fl), lambda i: (0, i, 0)),
            any_spec,
            any_spec,
        ],
        out_specs=pl.BlockSpec((tm, bc), lambda i: (i, 0)),
        scratch_shapes=[
            pltpu.VMEM((bc, F), jnp.bfloat16),
            pltpu.SemaphoreType.DMA((LANES,)),
        ],
        compiler_params=pltpu.CompilerParams(
            dimension_semantics=("arbitrary",), vmem_limit_bytes=48 * 1024 * 1024
        ),
        name="covariance_upper",
    )(slopes, slopes, colsl)


def solution(mesh):
    placed = (P("row", "col"), P("row", "col"), P("col", None), P("row"), P("col"))
    return jax.shard_map(
        functools.partial(per_device, mesh.shape["row"], mesh.shape["col"]),
        mesh=mesh, in_specs=placed, out_specs=P("row", "col"), check_vma=False,
    )
```

time: 441 us -> 258 us (0.59); the launches traced: 435 us -> 257 us
  waiting for transfers between devices: 354 us -> 0 us
  Pallas kernels: 0 us -> 244 us
  matrix products: 53.6 us -> 0 us
  between operations: 13.1 us -> 0.19 us
  starting transfers between devices: 5.56 us -> 0 us
  local copies, waits for them, and re-layouts: 6.07 us -> 11.3 us
    pallas_call x0 -> x2, Pallas kernels: none -> 244 us  [the longest x1 178 us: per_device(): pl.pallas_call(functools.partial(comm_kernel, C, R, rows, fl), out_shape=...]
    all_to_all x1 -> x0, waiting for transfers between devices: 164 us -> none  [per_device(): lax.all_to_all(gathered, 'col', split_axis=0, concat_axis=1, tiled=True)]
    reduce_scatter x1 -> x0, waiting for transfers between devices: 140 us -> none  [per_device(): lax.psum_scatter(product.astype(jnp.bfloat16), 'col', scatter_dimension=1...]
    dot_general x2 -> x0, matrix products: 53.6 us -> none  [the longest x1 42.8 us: per_device(): lax.dot_general(row_copy, columns, (((1,), (1,)), ((), ())), preferred_el...]
    all_gather x2 -> x0, waiting for transfers between devices: 49.2 us -> none  [the longest x1 32.8 us: per_device(): gathered = lax.all_gather(local_slopes, 'row', axis=0, tiled=True)]
    reshape x0 -> x1, local copies, waits for them, and re-layouts: none -> 5.77 us  [per_device(): rmask = rmask.reshape(C, rows, 1)]
    all_to_all x1 -> x0, starting transfers between devices: 5.47 us -> none  [per_device(): lax.all_to_all(gathered, 'col', split_axis=0, concat_axis=1, tiled=True)]
  transfers between devices with their start and end apart: 4 -> 0, of which waited for: 4 -> 0; matrix products, arithmetic and copies ran while one was open for 1% -> 0% of each run, Pallas kernels for 0% -> 0%
where the time goes in v1:
time: 258 us; the launch traced here: 257 us
  Pallas kernels  244 us (95%)
  local copies, waits for them, and re-layouts  11.3 us (4%)
    pallas_call x1, Pallas kernels, per_device(): pl.pallas_call(functools.partial(comm_kernel, C, R, rows, fl), out_shape=...  178 us
    pallas_call x1, Pallas kernels, per_device(): pl.pallas_call(functools.partial(cov_kernel, C, R, br, bc, F, tm, tn), gr...  66 us
    reshape x1, local copies, waits for them, and re-layouts, per_device(): rmask = rmask.reshape(C, rows, 1)  5.77 us

profile of v1, /device:TPU:17, one launch (start us, length us, event | category | flops | bytes accessed | tf_op | source)
XLA Modules:
  0.0 257.2 jit_solution(7473493055100078370)
XLA Ops:
  0.0 0.7 convert_element_type.14
  0.7 0.7 select_reduce_fusion
  1.4 0.6 broadcast_in_dim.30.fmask_ref
  2.0 0.1 broadcast_in_dim.16
  2.1 0.7 fusion.sel_ref
  2.8 2.8 %copy.7 = bf16[7680,64]{1,0:T(8,128)(2,1)} copy(bf16[7680,64]{0,1:T(8,128)(2,1)} %param.5) | data formatting | bytes 1966080 | tf_op args[0]
  5.6 5.8 %reshape.30.rmask_ref = f32[8,960,1]{2,1,0:T(8,128)} reshape(f32[60,128]{1,0:T(8,128)S(1)} %broadcast_in_dim.16) | data formatting | bytes 61440 | tf_op jit(solution)/shard_map/reshape | solution.py:337
  11.3 177.5 %slopes_ring.1 = (bf16[4,8,960,128]{3,2,1,0:T(8,128)(2,1)}, bf16[4,4,960,128]{3,2,1,0:T(8,128)(2,1)}) custom-call(bf16[8,960,640]{2,1,0:T(8,128)(2,1)} %bitcast.7, bf16[8,960,64]{2,1,0:T(8,128)(2,1)} %bitcast.8, bf16[640,512]{1,0:T(8,128)(2,1)} %cmd_ref.1, bf16[64,512]{1,0:T(8,128)(2,1)} %fusion.sel_ref, f32[8,960,1]{2,1,0:T(8,128)} %reshape.30.rmask_ref, ...), custom_call_target="tpu_custom_call" | custom-call | tf_op jit(solution)/shard_map/slopes_ring/pallas_call | solution.py:341
  188.8 0.0 copy-start
  188.9 2.1 copy-done
  191.0 66.0 %covariance_upper.1 = bf16[7680,3840]{1,0:T(8,128)(2,1)} custom-call(bf16[4,7680,128]{2,1,0:T(8,128)(2,1)} %bitcast.5, bf16[4,7680,128]{2,1,0:T(8,128)(2,1)} %bitcast.6, bf16[4,3840,128]{2,1,0:T(8,128)(2,1)S(1)} %bitcast.4), custom_call_target="tpu_custom_call" | custom-call | tf_op jit(solution)/shard_map/covariance_upper/pallas_call | solution.py:379
  (2 shorter events, 0.0 us)
Async XLA Ops:
  188.8 2.1 copy-start

commit v2 on v1

--- a/solution.py
+++ b/solution.py
@@ -31,9 +31,9 @@
 
 
 def comm_kernel(
-    C, R, rows, fl, inter_hbm, resid_hbm, cmd_ref, sel_ref, rmask_ref, fmask_ref,
+    C, R, rows, fl, inter_hbm, resid_hbm, cmd_ref, sv_ref, fv_ref,
     s_hbm, col_hbm,
-    inter, resid, stage, recv, own, fall,
+    inter, resid, stage, recv, own, fall, sel_ref, fmask_ref,
     in_sem, rs_send, rs_recv, ag_send, ag_recv, m_send, m_recv, c_send, c_recv, own_sem,
 ):
     r = lax.axis_index("row")
@@ -49,7 +49,13 @@
     nk = bc // rows
     tile = divisor(rows, 256, 16)
 
-    def load(k):
+    def chunk_of(q, row):
+        if C % 2:
+            return q
+        return q // 2 + lax.rem(q + row, 2) * (C // 2)
+
+    def load(q):
+        k = chunk_of(q, r)
         return (
             pltpu.make_async_copy(inter_hbm.at[k], inter.at[k], in_sem.at[0, k]),
             pltpu.make_async_copy(resid_hbm.at[k], resid.at[k], in_sem.at[1, k]),
@@ -80,6 +86,16 @@
         )
     pl.semaphore_wait(barrier, C - 1 + R - 1)
 
+    fc = resid.shape[2]
+    F = fmask_ref.shape[1]
+    frame_ids = lax.broadcasted_iota(jnp.int32, (fc, F), 1)
+    own_ids = c * fc + lax.broadcasted_iota(jnp.int32, (fc, F), 0)
+    sel_ref[...] = jnp.where(frame_ids == own_ids, 1.0, 0.0).astype(jnp.bfloat16)
+    valid = jnp.broadcast_to(fv_ref[...].astype(jnp.float32), (8, fc))
+    fmask_ref[...] = jnp.dot(
+        valid.astype(jnp.bfloat16), sel_ref[...], preferred_element_type=jnp.float32
+    )
+
     def mask_copy(j):
         return pltpu.make_async_remote_copy(
             src_ref=fmask_ref, dst_ref=fall.at[j - 1],
@@ -95,13 +111,13 @@
 
     def rs_chunk(l, s):
         if lane_is_up(l):
-            return lax.rem(p + 2 * C - 1 - s, C)
-        return lax.rem(p + 1 + s, C)
+            return chunk_of(lax.rem(p + 2 * C - 1 - s, C), r)
+        return chunk_of(lax.rem(p + 1 + s, C), r)
 
     def ag_chunk(l, s):
         if lane_is_up(l):
-            return lax.rem(p + 2 * C - s, C)
-        return lax.rem(p + s, C)
+            return chunk_of(lax.rem(p + 2 * C - s, C), r)
+        return chunk_of(lax.rem(p + s, C), r)
 
     def rs_copy(l, s):
         return pltpu.make_async_remote_copy(
@@ -164,16 +180,24 @@
             device_id=(r, nxt if lane_is_up(l) else prv), device_id_type=MESH,
         )
 
+    kp = chunk_of(p, r)
+    nb = sv_ref.shape[1]
+    valid_rows = sv_ref[...].astype(jnp.float32)
+
     def own_copy(l):
-        return pltpu.make_async_copy(own.at[l], s_hbm.at[l, p], own_sem.at[l])
+        return pltpu.make_async_copy(own.at[l], s_hbm.at[l, kp], own_sem.at[l])
 
     for l in range(LANES):
         rs_copy(l, C - 2).wait_recv()
 
         def last(t, _, l=l):
             at = pl.ds(pl.multiple_of(t * tile, 8), tile)
-            value = partial(l, p, t) + recv[l, C - 2, at, :].astype(jnp.float32)
-            value = value * rmask_ref[p, at, :] * frames[0:1, l * fl:(l + 1) * fl]
+            value = partial(l, kp, t) + recv[l, C - 2, at, :].astype(jnp.float32)
+            ids = kp * rows + t * tile + lax.broadcasted_iota(jnp.int32, (tile, nb), 0)
+            first = SBLK * lax.broadcasted_iota(jnp.int32, (tile, nb), 1)
+            inside = (ids >= first) & (ids < first + SBLK)
+            rmask = jnp.sum(jnp.where(inside, valid_rows, 0.0), axis=1, keepdims=True)
+            value = value * rmask * frames[0:1, l * fl:(l + 1) * fl]
             own[l, at, :] = value.astype(jnp.bfloat16)
             return 0
 
@@ -181,40 +205,45 @@
         ag_copy(l, 0, True).start()
         own_copy(l).start()
 
-    def down(l, k):
+    odd = lax.rem(r, 2) == 1
+    chip, root_chip = r // 2, rc // 2
+    child = (lax.rem(r + R - 1, R), lax.rem(chip * 2 + R - 1, R))
+    sends = (
+        (r <= rc) & odd,
+        (r <= rc) & (chip >= 1) & (odd | (r == rc)),
+    )
+    lag = 2 * (root_chip - chip) + jnp.where((r < rc) & jnp.logical_not(odd), 1, 0)
+
+    def down(b, l, k, from_slopes=False):
         return pltpu.make_async_remote_copy(
-            src_ref=col_hbm.at[l, k - k0], dst_ref=col_hbm.at[l, k - k0],
-            send_sem=c_send.at[l, k - k0], recv_sem=c_recv.at[l, k - k0],
-            device_id=(lax.rem(r + R - 1, R), c), device_id_type=MESH,
-        )
-
-    def down_first(l, k):
-        return pltpu.make_async_remote_copy(
-            src_ref=s_hbm.at[l, k], dst_ref=col_hbm.at[l, k - k0],
-            send_sem=c_send.at[l, k - k0], recv_sem=c_recv.at[l, k - k0],
-            device_id=(lax.rem(r + R - 1, R), c), device_id_type=MESH,
+            src_ref=s_hbm.at[l, k] if from_slopes else col_hbm.at[l, k - k0],
+            dst_ref=col_hbm.at[l, k - k0],
+            send_sem=c_send.at[b, l, k - k0], recv_sem=c_recv.at[l, k - k0],
+            device_id=(child[b], c), device_id_type=MESH,
         )
 
     def chain(u):
-        t = u - (rc - r)
+        t = u - lag
         for l in range(LANES):
             if lane_is_up(l):
-                k = lax.rem(p + 4 * C * R - t, C)
+                q = lax.rem(p + 4 * C * R - t, C)
             else:
-                k = lax.rem(p + 4 * C * R + t, C)
+                q = lax.rem(p + 4 * C * R + t, C)
+            k = chunk_of(q, rc)
             live = (t >= 0) & (t < C) & (r <= rc) & (k >= k0) & (k < k0 + nk)
 
             @pl.when(live & (r < rc))
             def _(l=l, k=k):
-                down(l, k).wait_recv()
-
-            @pl.when(live & (r > 0) & (r < rc))
-            def _(l=l, k=k):
-                down(l, k).start()
-
-            @pl.when(live & (r > 0) & (r == rc))
-            def _(l=l, k=k):
-                down_first(l, k).start()
+                down(0, l, k).wait_recv()
+
+            for b in range(2):
+                @pl.when(live & (r < rc) & sends[b])
+                def _(l=l, k=k, b=b):
+                    down(b, l, k).start()
+
+                @pl.when(live & (r == rc) & sends[b])
+                def _(l=l, k=k, b=b):
+                    down(b, l, k, True).start()
 
     for l in range(LANES):
         own_copy(l).wait()
@@ -245,9 +274,10 @@
 
     def drain_down(i, _):
         for l in range(LANES):
-            @pl.when((r > 0) & (r <= rc))
-            def _(l=l):
-                down(l, k0 + i).wait_send()
+            for b in range(2):
+                @pl.when(sends[b])
+                def _(l=l, b=b):
+                    down(b, l, k0 + i).wait_send()
         return 0
 
     lax.fori_loop(0, nk, drain_down, 0)
@@ -290,30 +320,46 @@
                 cp.wait()
 
     row0 = r * br + i * tm
-    for j in range(bc // tn):
-        col0 = c * bc + j * tn
-        at = slice(j * tn, (j + 1) * tn)
-
-        @pl.when(row0 >= col0 + tn)
-        def _(at=at):
+    col_base = c * bc
+    spans = [(j * tn, slice(j * tn, (j + 1) * tn)) for j in range(bc // tn)]
+
+    def value(at):
+        a = jnp.concatenate([rows_ref[l] for l in range(LANES)], axis=1)
+        return lax.dot_general(
+            a, cols[at, :], (((1,), (1,)), ((), ())), preferred_element_type=jnp.float32
+        ) / F
+
+    above = row0 + tm <= col_base
+    below = row0 >= col_base + bc
+
+    @pl.when(above)
+    def _():
+        for _, at in spans:
+            out_ref[:, at] = value(at).astype(jnp.bfloat16)
+
+    @pl.when(below)
+    def _():
+        for _, at in spans:
             out_ref[:, at] = jnp.zeros((tm, tn), jnp.bfloat16)
 
-        def value(at=at):
-            a = jnp.concatenate([rows_ref[l] for l in range(LANES)], axis=1)
-            return lax.dot_general(
-                a, cols[at, :], (((1,), (1,)), ((), ())),
-                preferred_element_type=jnp.float32,
-            ) / F
-
-        @pl.when(row0 + tm <= col0)
-        def _(at=at, value=value):
-            out_ref[:, at] = value().astype(jnp.bfloat16)
-
-        @pl.when((row0 < col0 + tn) & (row0 + tm > col0))
-        def _(at=at, value=value, col0=col0):
-            rid = row0 + lax.broadcasted_iota(jnp.int32, (tm, tn), 0)
-            cid = col0 + lax.broadcasted_iota(jnp.int32, (tm, tn), 1)
-            out_ref[:, at] = jnp.where(rid <= cid, value(), 0.0).astype(jnp.bfloat16)
+    @pl.when(jnp.logical_not(above | below))
+    def _():
+        for off, at in spans:
+            col0 = col_base + off
+
+            @pl.when(row0 >= col0 + tn)
+            def _(at=at):
+                out_ref[:, at] = jnp.zeros((tm, tn), jnp.bfloat16)
+
+            @pl.when(row0 + tm <= col0)
+            def _(at=at):
+                out_ref[:, at] = value(at).astype(jnp.bfloat16)
+
+            @pl.when((row0 < col0 + tn) & (row0 + tm > col0))
+            def _(at=at, col0=col0):
+                rid = row0 + lax.broadcasted_iota(jnp.int32, (tm, tn), 0)
+                cid = col0 + lax.broadcasted_iota(jnp.int32, (tm, tn), 1)
+                out_ref[:, at] = jnp.where(rid <= cid, value(at), 0.0).astype(jnp.bfloat16)
 
 
 def per_device(R, C, residual, interaction, commands, slope_valid, frame_valid):
@@ -323,18 +369,6 @@
     rows = br // C
     fl = F // LANES
     bc = br * R // C
-    c = lax.axis_index("col")
-    own_col = (
-        c * fc + jnp.arange(fc, dtype=jnp.int32)[:, None]
-        == jnp.arange(F, dtype=jnp.int32)[None, :]
-    )
-    sel = own_col.astype(jnp.bfloat16)
-    fmask = jnp.sum(
-        jnp.where(own_col, frame_valid[:, None], 0), axis=0, dtype=jnp.int32
-    ).astype(jnp.float32)
-    fmask = jnp.broadcast_to(fmask[None, :], (8, F))
-    rmask = jnp.broadcast_to(slope_valid.astype(jnp.float32)[:, None], (br // SBLK, SBLK))
-    rmask = rmask.reshape(C, rows, 1)
     any_spec = pl.BlockSpec(memory_space=pl.ANY)
     vmem = pl.BlockSpec(memory_space=pltpu.VMEM)
     nk = bc // rows
@@ -344,7 +378,7 @@
             jax.ShapeDtypeStruct((LANES, C, rows, fl), jnp.bfloat16),
             jax.ShapeDtypeStruct((LANES, nk, rows, fl), jnp.bfloat16),
         ],
-        in_specs=[any_spec, any_spec, vmem, vmem, vmem, vmem],
+        in_specs=[any_spec, any_spec, vmem, vmem, vmem],
         out_specs=[any_spec, any_spec],
         scratch_shapes=[
             pltpu.VMEM((C, rows, kd), jnp.bfloat16),
@@ -353,6 +387,8 @@
             pltpu.VMEM((LANES, C - 1, rows, fl), jnp.bfloat16),
             pltpu.VMEM((LANES, rows, fl), jnp.bfloat16),
             pltpu.VMEM((C - 1, 8, F), jnp.float32),
+            pltpu.VMEM((fc, F), jnp.bfloat16),
+            pltpu.VMEM((8, F), jnp.float32),
             pltpu.SemaphoreType.DMA((2, C)),
             pltpu.SemaphoreType.DMA((LANES, C - 1)),
             pltpu.SemaphoreType.DMA((LANES, C - 1)),
@@ -360,7 +396,7 @@
             pltpu.SemaphoreType.DMA((LANES, C - 1)),
             pltpu.SemaphoreType.DMA((C - 1,)),
             pltpu.SemaphoreType.DMA((C - 1,)),
-            pltpu.SemaphoreType.DMA((LANES, nk)),
+            pltpu.SemaphoreType.DMA((2, LANES, nk)),
             pltpu.SemaphoreType.DMA((LANES, nk)),
             pltpu.SemaphoreType.DMA((LANES,)),
         ],
@@ -370,11 +406,11 @@
         name="slopes_ring",
     )(
         interaction.reshape(C, rows, kd), residual.reshape(C, rows, fc),
-        commands, sel, rmask, fmask,
+        commands, slope_valid[None, :], frame_valid[None, :],
     )
     slopes = slopes.reshape(LANES, br, fl)
     colsl = colsl.reshape(LANES, bc, fl)
-    tm = divisor(br, 256, 16)
+    tm = divisor(br, 768, 16)
     tn = divisor(bc, 768, 128)
     return pl.pallas_call(
         functools.partial(cov_kernel, C, R, br, bc, F, tm, tn),
@@ -391,7 +427,7 @@
             pltpu.SemaphoreType.DMA((LANES,)),
         ],
         compiler_params=pltpu.CompilerParams(
-            dimension_semantics=("arbitrary",), vmem_limit_bytes=48 * 1024 * 1024
+            dimension_semantics=("arbitrary",), vmem_limit_bytes=62 * 1024 * 1024
         ),
         name="covariance_upper",
     )(slopes, slopes, colsl)

time: 258 us -> 210 us (0.81)
  Pallas kernels: 244 us -> 207 us
  local copies, waits for them, and re-layouts: 11.3 us -> 2.67 us
    pallas_call x1, Pallas kernels: 66 us -> 39.3 us  [per_device(): pl.pallas_call(functools.partial(cov_kernel, C, R, br, bc, F, tm, tn), gr...]
    pallas_call x1, Pallas kernels: 178 us -> 167 us  [per_device(): pl.pallas_call(functools.partial(comm_kernel, C, R, rows, fl), out_shape=...]
    reshape x1 -> x0, local copies, waits for them, and re-layouts: 5.77 us -> none  [per_device(): rmask = rmask.reshape(C, rows, 1)]
where the time goes in v2:
time: 210 us
  Pallas kernels  207 us (99%)
  local copies, waits for them, and re-layouts  2.67 us (1%)
    pallas_call x1, Pallas kernels, per_device(): pl.pallas_call(functools.partial(comm_kernel, C, R, rows, fl), out_shape=...  167 us
    pallas_call x1, Pallas kernels, per_device(): pl.pallas_call(functools.partial(cov_kernel, C, R, br, bc, F, tm, tn), gr...  39.3 us

profile of v2, /device:TPU:17, one launch (start us, length us, event | category | flops | bytes accessed | tf_op | source)
XLA Modules:
  0.0 209.6 jit_solution(5685369192750899009)
XLA Ops:
  0.0 2.7 %copy.6 = bf16[7680,64]{1,0:T(8,128)(2,1)} copy(bf16[7680,64]{0,1:T(8,128)(2,1)} %param.5) | data formatting | bytes 1966080 | tf_op args[0]
  2.7 167.4 %slopes_ring.1 = (bf16[4,8,960,128]{3,2,1,0:T(8,128)(2,1)}, bf16[4,4,960,128]{3,2,1,0:T(8,128)(2,1)}) custom-call(bf16[8,960,640]{2,1,0:T(8,128)(2,1)} %bitcast.8, bf16[8,960,64]{2,1,0:T(8,128)(2,1)} %bitcast.9, bf16[640,512]{1,0:T(8,128)(2,1)} %cmd_ref.1, s32[1,60]{1,0:T(1,128)} %bitcast.11, s32[1,64]{1,0:T(1,128)} %bitcast.12), custom_call_target="tpu_custom_call" | custom-call | tf_op jit(solution)/shard_map/slopes_ring/pallas_call | solution.py:375
  170.1 39.3 %covariance_upper.1 = bf16[7680,3840]{1,0:T(8,128)(2,1)} custom-call(bf16[4,7680,128]{2,1,0:T(8,128)(2,1)} %bitcast.6, bf16[4,7680,128]{2,1,0:T(8,128)(2,1)} %bitcast.7, bf16[4,3840,128]{2,1,0:T(8,128)(2,1)} %bitcast.10), custom_call_target="tpu_custom_call" | custom-call | tf_op jit(solution)/shard_map/covariance_upper/pallas_call | solution.py:415

commit v3 on v2

--- a/solution.py
+++ b/solution.py
@@ -33,8 +33,8 @@
 def comm_kernel(
     C, R, rows, fl, inter_hbm, resid_hbm, cmd_ref, sv_ref, fv_ref,
     s_hbm, col_hbm,
-    inter, resid, stage, recv, own, fall, sel_ref, fmask_ref,
-    in_sem, rs_send, rs_recv, ag_send, ag_recv, m_send, m_recv, c_send, c_recv, own_sem,
+    inter, resid_t, resid, stage, recv, own, fall, sel_ref, fmask_ref,
+    in_sem, rs_send, rs_recv, ag_send, ag_recv, m_send, m_recv, c_send, c_recv, own_sem, resid_sem,
 ):
     r = lax.axis_index("row")
     c = lax.axis_index("col")
@@ -56,37 +56,32 @@
 
     def load(q):
         k = chunk_of(q, r)
-        return (
-            pltpu.make_async_copy(inter_hbm.at[k], inter.at[k], in_sem.at[0, k]),
-            pltpu.make_async_copy(resid_hbm.at[k], resid.at[k], in_sem.at[1, k]),
-        )
+        return pltpu.make_async_copy(inter_hbm.at[k], inter.at[k], in_sem.at[k])
 
     def start_load(k):
-        for cp in load(k):
-            cp.start()
+        load(k).start()
 
     def wait_load(k):
-        for cp in load(k):
-            cp.wait()
-
+        load(k).wait()
+
+    barrier = pltpu.get_barrier_semaphore()
+    for j in range(1, C):
+        pl.semaphore_signal(
+            barrier, inc=1, device_id=(r, lax.rem(c + j, C)), device_id_type=MESH
+        )
+    for j in range(1, R):
+        pl.semaphore_signal(
+            barrier, inc=1, device_id=(lax.rem(r + j, R), c), device_id_type=MESH
+        )
+    resid_copy = pltpu.make_async_copy(resid_hbm, resid_t, resid_sem)
+    resid_copy.start()
     for i in range(1, C // 2):
         start_load(lax.rem(p + C - i, C))
         start_load(lax.rem(p + i, C))
     start_load(lax.rem(p + C // 2, C))
     start_load(p)
 
-    barrier = pltpu.get_barrier_semaphore()
-    for j in range(1, C):
-        pl.semaphore_signal(
-            barrier, inc=1, device_id=(r, lax.rem(c + j, C)), device_id_type=MESH
-        )
-    for j in range(1, R):
-        pl.semaphore_signal(
-            barrier, inc=1, device_id=(lax.rem(r + j, R), c), device_id_type=MESH
-        )
-    pl.semaphore_wait(barrier, C - 1 + R - 1)
-
-    fc = resid.shape[2]
+    fc = resid.shape[1]
     F = fmask_ref.shape[1]
     frame_ids = lax.broadcasted_iota(jnp.int32, (fc, F), 1)
     own_ids = c * fc + lax.broadcasted_iota(jnp.int32, (fc, F), 0)
@@ -103,11 +98,18 @@
             device_id=(r, lax.rem(c + j, C)), device_id_type=MESH,
         )
 
-    for j in range(1, C):
-        mask_copy(j).start()
+    resid_copy.wait()
+    width = divisor(br, 512, 128)
+
+    def turn(i, _):
+        at = pl.ds(pl.multiple_of(i * width, 128), width)
+        resid[at, :] = resid_t[:, at].astype(jnp.float32).T
+        return 0
+
+    lax.fori_loop(0, br // width, turn, 0)
 
     def lane_is_up(l):
-        return l < LANES // 2
+        return l % 2 == 0
 
     def rs_chunk(l, s):
         if lane_is_up(l):
@@ -132,7 +134,9 @@
         return jnp.dot(
             inter[k, at, :], cmd_ref[:, cols], preferred_element_type=jnp.float32
         ) + jnp.dot(
-            resid[k, at, :], sel_ref[:, cols], preferred_element_type=jnp.float32
+            resid[pl.ds(pl.multiple_of(k * rows + t * tile, 8), tile), :].astype(jnp.bfloat16),
+            sel_ref[:, cols],
+            preferred_element_type=jnp.float32
         )
 
     def rs_step(s, first):
@@ -150,7 +154,14 @@
                 return 0
 
             lax.fori_loop(0, rows // tile, one, 0)
-            rs_copy(l, s).start()
+            if not first:
+                rs_copy(l, s).start()
+        if first:
+            pl.semaphore_wait(barrier, C - 1 + R - 1)
+            for l in range(LANES):
+                rs_copy(l, s).start()
+            for j in range(1, C):
+                mask_copy(j).start()
 
     for s in range(C - 1):
         i = s + 1
@@ -206,13 +217,14 @@
         own_copy(l).start()
 
     odd = lax.rem(r, 2) == 1
+    main = lax.rem(r, 2) == lax.rem(rc, 2)
     chip, root_chip = r // 2, rc // 2
-    child = (lax.rem(r + R - 1, R), lax.rem(chip * 2 + R - 1, R))
+    child = (chip * 2 + 1 - lax.rem(r, 2), lax.rem(r + R - 2, R))
     sends = (
-        (r <= rc) & odd,
-        (r <= rc) & (chip >= 1) & (odd | (r == rc)),
+        main & ((r < rc) | ((r == rc) & odd)),
+        main & (r <= rc) & (chip >= 1),
     )
-    lag = 2 * (root_chip - chip) + jnp.where((r < rc) & jnp.logical_not(odd), 1, 0)
+    lag = 2 * (root_chip - chip) + jnp.where(main, 0, 1)
 
     def down(b, l, k, from_slopes=False):
         return pltpu.make_async_remote_copy(
@@ -382,14 +394,15 @@
         out_specs=[any_spec, any_spec],
         scratch_shapes=[
             pltpu.VMEM((C, rows, kd), jnp.bfloat16),
-            pltpu.VMEM((C, rows, fc), jnp.bfloat16),
+            pltpu.VMEM((fc, br), jnp.bfloat16),
+            pltpu.VMEM((br, fc), jnp.float32),
             pltpu.VMEM((LANES, C - 1, rows, fl), jnp.bfloat16),
             pltpu.VMEM((LANES, C - 1, rows, fl), jnp.bfloat16),
             pltpu.VMEM((LANES, rows, fl), jnp.bfloat16),
             pltpu.VMEM((C - 1, 8, F), jnp.float32),
             pltpu.VMEM((fc, F), jnp.bfloat16),
             pltpu.VMEM((8, F), jnp.float32),
-            pltpu.SemaphoreType.DMA((2, C)),
+            pltpu.SemaphoreType.DMA((C,)),
             pltpu.SemaphoreType.DMA((LANES, C - 1)),
             pltpu.SemaphoreType.DMA((LANES, C - 1)),
             pltpu.SemaphoreType.DMA((LANES, C - 1)),
@@ -399,13 +412,14 @@
             pltpu.SemaphoreType.DMA((2, LANES, nk)),
             pltpu.SemaphoreType.DMA((LANES, nk)),
             pltpu.SemaphoreType.DMA((LANES,)),
+            pltpu.SemaphoreType.DMA,
         ],
         compiler_params=pltpu.CompilerParams(
             collective_id=0, has_side_effects=True, vmem_limit_bytes=56 * 1024 * 1024
         ),
         name="slopes_ring",
     )(
-        interaction.reshape(C, rows, kd), residual.reshape(C, rows, fc),
+        interaction.reshape(C, rows, kd), residual.T,
         commands, slope_valid[None, :], frame_valid[None, :],
     )
     slopes = slopes.reshape(LANES, br, fl)

time: 210 us -> 210 us (level)
  Pallas kernels: 207 us -> 210 us
  local copies, waits for them, and re-layouts: 2.67 us -> 0 us
    pallas_call x1, Pallas kernels: 167 us -> 170 us  [per_device(): pl.pallas_call(functools.partial(comm_kernel, C, R, rows, fl), out_shape=...]
    unnamed x1 -> x0, local copies, waits for them, and re-layouts: 2.67 us -> none
where the time goes in v3:
time: 210 us
  Pallas kernels  210 us (100%)
    pallas_call x1, Pallas kernels, per_device(): pl.pallas_call(functools.partial(comm_kernel, C, R, rows, fl), out_shape=...  170 us
    pallas_call x1, Pallas kernels, per_device(): pl.pallas_call(functools.partial(cov_kernel, C, R, br, bc, F, tm, tn), gr...  39.3 us

profile of v3, /device:TPU:17, one launch (start us, length us, event | category | flops | bytes accessed | tf_op | source)
XLA Modules:
  0.0 209.9 jit_solution(4901815161073878709)
XLA Ops:
  0.0 170.5 %slopes_ring.1 = (bf16[4,8,960,128]{3,2,1,0:T(8,128)(2,1)}, bf16[4,4,960,128]{3,2,1,0:T(8,128)(2,1)}) custom-call(bf16[8,960,640]{2,1,0:T(8,128)(2,1)} %bitcast.8, bf16[64,7680]{1,0:T(8,128)(2,1)} %bitcast.10, bf16[640,512]{1,0:T(8,128)(2,1)} %cmd_ref.1, s32[1,60]{1,0:T(1,128)} %bitcast.11, s32[1,64]{1,0:T(1,128)} %bitcast.12), custom_call_target="tpu_custom_call" | custom-call | tf_op jit(solution)/shard_map/slopes_ring/pallas_call | solution.py:387
  170.5 39.3 %covariance_upper.1 = bf16[7680,3840]{1,0:T(8,128)(2,1)} custom-call(bf16[4,7680,128]{2,1,0:T(8,128)(2,1)} %bitcast.6, bf16[4,7680,128]{2,1,0:T(8,128)(2,1)} %bitcast.7, bf16[4,3840,128]{2,1,0:T(8,128)(2,1)} %bitcast.9), custom_call_target="tpu_custom_call" | custom-call | tf_op jit(solution)/shard_map/covariance_upper/pallas_call | solution.py:429
